TPU v7x, 32 devices: a whole 2x2x4 slice. The times are simulated.
32 devices in a mesh: row: 8 (over z, x), col: 4 (over y, core).
Axes of the slice: x: 2, y: 2, z: 4, core: 2. Of those that a mesh axis runs over, the one named last changes fastest.
Arguments:
- x_first: bfloat16 [768, 18432], P(None, ('row', 'col')), may hold values from -1.5 to 1.5
- x_second: bfloat16 [768, 18432], P(None, ('row', 'col')), may hold values from -1.5 to 1.5
- w_first: bfloat16 [18432, 256], P(('row', 'col')), may hold values from -12 to 12
- w_second: bfloat16 [18432, 256], P(('row', 'col')), may hold values from -12 to 12
- counts: int32 [2], replicated, may hold values from 384 to 768
- damping: float32 [1], replicated, may hold values from 0.2 to 0.6
- eig_low: float32 [1], replicated, may hold values from 0.1 to 0.4
- eig_high: float32 [1], replicated, may hold values from 3 to 6
Outputs:
- merged: float32 [18432, 256], P(('row', 'col'))
- residual: float32 [18432, 256], P(('row', 'col'))
Inputs may be any that keep to these rules, and one draw needn't show every extreme that they name: counts[i] is how many leading rows of domain i are used; later rows are ignored.
All inputs are finite; a program needn't handle non-finite values.
Results may differ from a plain program's by a relative error of at most 0.0003.
Values may be sent and summed in bfloat16 or wider, within the bound.
A program may use at most 64 MiB of HBM per device.

v0:
```python
import jax
import jax.numpy as jnp
from jax import lax
from jax.sharding import PartitionSpec as P

ITERS = 2


CONTRACT = (((0,), (0,)), ((), ()))


def back_project(dense, summed):
    return lax.dot_general(
        dense, summed, CONTRACT, precision=lax.Precision.HIGHEST, preferred_element_type=jnp.float32
    )


def high_dot(left, right):
    return jnp.dot(left, right, precision=lax.Precision.HIGHEST, preferred_element_type=jnp.float32)


def body(x_first, x_second, w_first, w_second, counts, damping, eig_low, eig_high):
    act_rows = x_first.shape[0]
    position = lax.iota(jnp.int32, act_rows)
    masked_first = x_first * (position < counts[0]).astype(jnp.bfloat16)[:, None]
    masked_second = x_second * (position < counts[1]).astype(jnp.bfloat16)[:, None]
    scale_first = 1.0 / counts[0].astype(jnp.float32)
    scale_second = 1.0 / counts[1].astype(jnp.float32)
    ridge = damping[0]
    dense_first = masked_first.astype(jnp.float32)
    dense_second = masked_second.astype(jnp.float32)
    proj_first, proj_second = lax.psum(
        (
            jnp.dot(masked_first, w_first, preferred_element_type=jnp.float32),
            jnp.dot(masked_second, w_second, preferred_element_type=jnp.float32),
        ),
        ("row", "col"),
    )
    rhs = (
        back_project(dense_first, proj_first) * scale_first
        + back_project(dense_second, proj_second) * scale_second
    )
    middle = (eig_high[0] + eig_low[0]) / 2.0
    radius = (eig_high[0] - eig_low[0]) / 2.0
    sigma = middle / radius
    rho_now = 1.0 / sigma
    merged = jnp.zeros_like(rhs)
    residual = rhs
    direction = rhs / middle
    for step_index in range(ITERS):
        sum_first, sum_second = lax.psum(
            (high_dot(dense_first, direction), high_dot(dense_second, direction)), ("row", "col")
        )
        image = (
            back_project(dense_first, sum_first) * scale_first
            + back_project(dense_second, sum_second) * scale_second
            + ridge * direction
        )
        merged = merged + direction
        residual = residual - image
        if step_index + 1 < ITERS:
            rho_new = 1.0 / (2.0 * sigma - rho_now)
            direction = rho_new * rho_now * direction + 2.0 * rho_new / radius * residual
            rho_now = rho_new
    return (merged, residual)


def solution(mesh):
    return jax.shard_map(
        body,
        mesh=mesh,
        in_specs=(
            P(None, ("row", "col")),
            P(None, ("row", "col")),
            P(("row", "col"), None),
            P(("row", "col"), None),
            P(),
            P(),
            P(),
            P(),
        ),
        out_specs=(P(("row", "col"), None), P(("row", "col"), None)),
        check_vma=False,
    )
```

profile of v0, /device:TPU:0, one launch (start us, length us, event | category | flops | bytes accessed | tf_op | source)
XLA Modules:
  0.0 440.3 jit_solution(8547836377722885498)
XLA Ops:
  7.2 0.0 copy-start
  7.2 0.0 all-reduce.11.cloned.1.call-start
  7.2 1.3 fusion.16
  8.5 0.6 fusion.14
  9.2 0.7 fusion.13
  9.9 0.0 copy-done
  9.9 0.0 copy-start.2
  9.9 0.0 copy-start.6
  9.9 2.7 fusion.9
  12.5 0.0 copy-done.2
  12.5 0.0 copy-done.6
  12.6 1.4 fusion.12
  14.0 0.0 all-reduce.11.cloned.1.call-update
  14.0 0.0 all-reduce.9.cloned.1.call-start
  16.8 133.0 %all-reduce.11.cloned.1.call-done = (f32[768,256]{1,0:T(8,128)}, f32[768,256]{1,0:T(8,128)}) async-done(((f32[768,256]{1,0:T(8,128)}, f32[768,256]{1,0:T(8,128)}), (f32[768,256]{1,0:T(8,128)}, f32[768,256]{1,0:T(8,128)})) %all-reduce.11.cloned.1.call-update) | async-done | bytes 1572880 | tf_op jit(solution)/shard_map/psum | solution.py:32
  149.8 0.0 copy-done.1
  149.8 2.1 convolution_multiply_fusion.5
  151.9 0.0 copy-done.3
  151.9 0.9 fusion.6
  152.9 2.2 fusion.11
  155.1 2.2 fusion.8
  157.3 0.0 all-reduce.9.cloned.1.call-update
  157.3 0.2 all-reduce.7.cloned.1.call-start
  158.4 130.9 %all-reduce.9.cloned.1.call-done = (f32[768,256]{1,0:T(8,128)}, f32[768,256]{1,0:T(8,128)}) async-done(((f32[768,256]{1,0:T(8,128)}, f32[768,256]{1,0:T(8,128)}), (f32[768,256]{1,0:T(8,128)}, f32[768,256]{1,0:T(8,128)})) %all-reduce.9.cloned.1.call-update) | async-done | bytes 1572880 | tf_op jit(solution)/shard_map/psum | solution.py:51
  289.3 2.1 convolution_multiply_fusion.3
  291.4 1.9 fusion.15
  293.3 2.3 fusion.10
  295.6 2.3 fusion.7
  297.9 0.0 all-reduce.7.cloned.1.call-update
  297.9 131.9 %all-reduce.7.cloned.1.call-done = (f32[768,256]{1,0:T(8,128)}, f32[768,256]{1,0:T(8,128)}) async-done(((f32[768,256]{1,0:T(8,128)}, f32[768,256]{1,0:T(8,128)}), (f32[768,256]{1,0:T(8,128)}, f32[768,256]{1,0:T(8,128)})) %all-reduce.7.cloned.1.call-update) | async-done | bytes 1572880 | tf_op jit(solution)/shard_map/psum | solution.py:51
  429.8 2.1 convolution_multiply_fusion.1
  432.0 1.8 fusion.2
  (6 shorter events, 0.0 us)
Async XLA Ops:
  7.2 2.7 copy-start
  7.2 142.6 %all-reduce.11.cloned.1.call-start = ((), (), s32[]{:S(2)}) async-start(), calls=%async_computation.2 | async-start | bytes 3145728 | tf_op jit(solution)/shard_map/psum | solution.py:32
  9.9 2.7 copy-start.2
  9.9 2.7 copy-start.6
  14.0 135.8 %copy-start.1 = (bf16[768,576]{0,1:T(8,128)(2,1)S(1)}, bf16[768,576]{0,1:T(8,128)(2,1)}, u32[]{:S(2)}) copy-start(bf16[768,576]{0,1:T(8,128)(2,1)} %param.8) | copy-start | bytes 2654212
  14.0 275.3 %all-reduce.9.cloned.1.call-start = ((), (), s32[]{:S(2)}) async-start(), calls=%async_computation.1 | async-start | bytes 3145728 | tf_op jit(solution)/shard_map/psum | solution.py:51
  149.8 2.1 copy-start.3
  157.3 272.5 %all-reduce.7.cloned.1.call-start = ((), (), s32[]{:S(2)}) async-start(), calls=%async_computation | async-start | bytes 3145728 | tf_op jit(solution)/shard_map/psum | solution.py:51
  289.3 2.1 copy-start.4
  429.8 2.1 copy-start.5
Sparse Core Ops, SparseCore 0:
  14.1 135.6 all-reduce.10
  157.4 131.8 all-reduce.8
  298.0 131.7 all-reduce.6
where the time goes:
time: 441 us; the launch traced here: 440 us
  waiting for transfers between devices  396 us (90%)
  matrix products  24.1 us (5%)
  between operations  17.4 us (4%)
    psum x2, waiting for transfers between devices, body(): lax.psum((high_dot(dense_first, direction), high_dot(dense_second, direct...  263 us
    psum x1, waiting for transfers between devices, body(): lax.psum((jnp.dot(masked_first, w_first, preferred_element_type=jnp.float...  133 us
    dot_general x6, matrix products, back_project(): lax.dot_general(dense, summed, CONTRACT, precision=lax.Precision.HIGHEST,...  11 us
    dot_general x4, matrix products, high_dot(): jnp.dot(left, right, precision=lax.Precision.HIGHEST, preferred_element_t...  8.96 us
  transfers between devices with their start and end apart: 3, of which 3 were waited for; matrix products, arithmetic and copies ran while one was open for 0% of the time, Pallas kernels for 0%

commit v1 on v0

v1 whole, which is shorter than its diff:
```python
import functools

import jax
import jax.numpy as jnp
from jax import lax
from jax.experimental import pallas as pl
from jax.experimental.pallas import tpu as pltpu
from jax.sharding import PartitionSpec as P

ITERS = 2
HALVES = 2
LANES = 128
SUBLANES = 8
REDUCTIONS = ITERS + 1


def axis_groups(name, size):
    pair = 2 if size % 2 == 0 else 1
    found = [(name, 1, pair), (name, pair, size // pair)]
    return [group for group in found if group[2] > 1]


def plan(mesh_shape, rows):
    col = axis_groups("col", mesh_shape["col"])
    row = axis_groups("row", mesh_shape["row"])
    orders = [col[:1] + row[:1] + col[1:] + row[1:], col[:1] + col[1:] + row[:1] + row[1:]]
    result = []
    for order in orders:
        height, stages = rows, []
        for group in order:
            members = group[2]
            split = height % (members * SUBLANES) == 0
            chunk = height // members if split else height
            stages.append((group, height, chunk, split))
            height = chunk
        result.append(stages)
    return result


def member_of(group):
    name, stride, members = group
    return lax.rem(lax.div(lax.axis_index(name), stride), members)


def peer_at(group, offset):
    name, stride, members = group
    me = member_of(group)
    other = lax.rem(me + offset, members)
    return {name: lax.axis_index(name) + (other - me) * stride}, other


def kernel(
    stages_of, groups, counts, damping, eig_low, eig_high, x_first, x_second, w_first, w_second,
    merged, residual, dense, sums, full, d_zero, rest, high, low, q_high, q_low, *more,
):
    landing = more[: len(stages_of)]
    send_sem, recv_sem = more[len(stages_of) :]
    rows = x_first.shape[0]
    per_part = [sum(group[2] - 1 for group, _, _, _ in stages) for stages in stages_of]
    most = max(per_part)

    barrier = pltpu.get_barrier_semaphore()
    partners = 0
    for group in groups:
        for offset in range(1, group[2]):
            pl.semaphore_signal(
                barrier, inc=1, device_id=peer_at(group, offset)[0], device_id_type=pl.DeviceIdType.MESH
            )
            partners += 1

    def lane(value):
        return jnp.full((1, LANES), value, jnp.float32)

    scales = [1.0 / lane(counts[i].astype(jnp.float32)) for i in range(2)]
    ridge = lane(damping[0])
    middle = (lane(eig_high[0]) + lane(eig_low[0])) / 2.0
    radius = (lane(eig_high[0]) - lane(eig_low[0])) / 2.0
    sigma = middle / radius

    position = lax.broadcasted_iota(jnp.int32, x_first.shape, 0)
    for domain, source in enumerate((x_first, x_second)):
        value = source[...].astype(jnp.float32)
        dense[pl.ds(domain * rows, rows), :] = jnp.where(position < counts[domain], value, 0.0).astype(jnp.bfloat16)

    def reduce_all(index, produce):
        sent = []
        parts = [(domain, half) for domain in range(2) for half in range(HALVES)]

        def start(part, phase, slot, src, dst, device):
            at = (index * 2 + phase, part, slot)
            copy = pltpu.make_async_remote_copy(
                src_ref=src, dst_ref=dst, send_sem=send_sem.at[at], recv_sem=recv_sem.at[at],
                device_id=device, device_id_type=pl.DeviceIdType.MESH,
            )
            copy.start()
            return copy

        state = {}

        def launch_scatter(part, stage):
            domain, half = parts[part]
            group, height, chunk, split = stages_of[half][stage]
            base = state[part]["base"]
            slot0 = state[part]["slot"]
            copies = []
            for offset in range(1, group[2]):
                device, other = peer_at(group, offset)
                begin = base + other * chunk if split else base
                begin = pl.multiple_of(begin, SUBLANES)
                spot = state[part]["spot"] + (offset - 1) * chunk
                copies.append(
                    start(
                        part, 0, slot0 + offset - 1,
                        sums.at[half, pl.ds(domain * rows + begin, chunk), :],
                        landing[half].at[index, domain, pl.ds(spot, chunk), :],
                        device,
                    )
                )
            if split:
                sent.extend(copies)
            state[part]["wait"] = copies

        def finish_scatter(part, stage):
            domain, half = parts[part]
            group, height, chunk, split = stages_of[half][stage]
            st = state[part]
            st["bases"].append(st["base"])
            if split:
                st["base"] = st["base"] + member_of(group) * chunk
            own = pl.ds(pl.multiple_of(domain * rows + st["base"], SUBLANES), chunk)
            last = stage == len(stages_of[half]) - 1
            if not split:
                for copy in st["wait"]:
                    copy.wait_send()
            for copy in st["wait"]:
                copy.wait_recv()
            total = sums[half, own, :]
            for offset in range(1, group[2]):
                total = total + landing[half][index, domain, pl.ds(st["spot"] + (offset - 1) * chunk, chunk), :]
            if last:
                full[index, half, own, :] = total
            else:
                sums[half, own, :] = total
            st["spot"] += (group[2] - 1) * chunk
            st["slot"] += group[2] - 1

        def launch_gather(part, stage):
            domain, half = parts[part]
            group, height, chunk, split = stages_of[half][stage]
            st = state[part]
            st["slot"] -= group[2] - 1
            copies = []
            if split:
                begin = pl.multiple_of(domain * rows + st["base"], SUBLANES)
                for offset in range(1, group[2]):
                    where = full.at[index, half, pl.ds(begin, chunk), :]
                    device, _ = peer_at(group, offset)
                    copies.append(start(part, 1, st["slot"] + offset - 1, where, where, device))
            st["base"] = st["bases"].pop()
            sent.extend(copies)
            st["wait"] = copies

        def finish_gather(part):
            for copy in state[part]["wait"]:
                copy.wait_recv()

        count = [len(stages_of[half]) for _, half in parts]
        for domain in range(2):
            produce(domain)
            if index == 0 and domain == 0:
                pl.semaphore_wait(barrier, partners)
            for half in range(HALVES):
                part = domain * HALVES + half
                state[part] = {"base": 0, "slot": 0, "spot": 0, "bases": []}
                launch_scatter(part, 0)
        for stage in range(max(count)):
            for part in range(len(parts)):
                if stage < count[part]:
                    finish_scatter(part, stage)
                    if stage + 1 < count[part]:
                        launch_scatter(part, stage + 1)
                    else:
                        launch_gather(part, stage)
        for stage in reversed(range(max(count))):
            for part in range(len(parts)):
                if stage < count[part]:
                    finish_gather(part)
                    if stage > 0:
                        launch_gather(part, stage - 1)
        return sent

    def settle(sent):
        for copy in sent:
            copy.wait_send()

    def split_store(domain, half, value):
        place = pl.ds(domain * rows, rows), pl.ds(half * LANES, LANES)
        top = value.astype(jnp.bfloat16)
        high[place] = top
        low[place] = (value - top.astype(jnp.float32)).astype(jnp.bfloat16)

    def back_project():
        contract = (((0,), (0,)), ((), ()))
        return lax.dot_general(
            dense[...], high[...], contract, preferred_element_type=jnp.float32
        ) + lax.dot_general(dense[...], low[...], contract, preferred_element_type=jnp.float32)

    def store_sums(domain, value):
        for half in range(HALVES):
            sums[half, pl.ds(domain * rows, rows), :] = value[:, half * LANES : (half + 1) * LANES]

    def first_product(domain):
        weights = (w_first, w_second)[domain]
        store_sums(
            domain,
            jnp.dot(dense[pl.ds(domain * rows, rows), :], weights[...], preferred_element_type=jnp.float32),
        )

    def next_product(domain):
        part = dense[pl.ds(domain * rows, rows), :]
        store_sums(
            domain,
            jnp.dot(part, q_high[...], preferred_element_type=jnp.float32)
            + jnp.dot(part, q_low[...], preferred_element_type=jnp.float32),
        )

    def project_and_sum(index):
        seen = back_project()
        top = seen.astype(jnp.bfloat16)
        q_high[...] = top
        q_low[...] = (seen - top.astype(jnp.float32)).astype(jnp.bfloat16)
        if index == 1:
            merged[...] = seen
        else:
            merged[...] = merged[...] + seen
        return reduce_all(index, next_product)

    sent = reduce_all(0, first_product)
    settle(sent)
    blocks = [(domain, half, pl.ds(domain * rows, rows)) for domain in range(2) for half in range(HALVES)]
    for domain, half, place in blocks:
        value = full[0, half, place, :] * scales[domain]
        rest[half, place, :] = value
        value = value / middle
        d_zero[half, place, :] = value
        split_store(domain, half, value)
    rho_now = 1.0 / sigma
    for step in range(ITERS):
        settle(project_and_sum(step + 1))
        rho_new = 1.0 / (2.0 * sigma - rho_now)
        for domain, half, place in blocks:
            direction = d_zero[half, place, :]
            left = rest[half, place, :] - (full[step + 1, half, place, :] * scales[domain] + ridge * direction)
            if step + 1 < ITERS:
                rest[half, place, :] = left
                direction = rho_new * rho_now * direction + (2.0 * rho_new / radius) * left
                d_zero[half, place, :] = direction
                split_store(domain, half, direction)
            else:
                split_store(domain, half, left)
        rho_now = rho_new
    residual[...] = back_project()


def solution(mesh):
    shape = dict(mesh.shape)

    def body(x_first, x_second, w_first, w_second, counts, damping, eig_low, eig_high):
        rows, features = x_first.shape
        columns = w_first.shape[1]
        stages_of = plan(shape, rows)
        groups = axis_groups("col", shape["col"]) + axis_groups("row", shape["row"])
        slots = max(sum(stage[0][2] - 1 for stage in stages) for stages in stages_of)
        spots = [sum((stage[0][2] - 1) * stage[2] for stage in stages) for stages in stages_of]
        smem = pl.BlockSpec(memory_space=pltpu.SMEM)
        vmem = pl.BlockSpec(memory_space=pltpu.VMEM)
        out = jax.ShapeDtypeStruct((features, columns), jnp.float32)
        wide = (HALVES, 2 * rows, LANES)
        semaphores = pltpu.SemaphoreType.DMA((REDUCTIONS * 2, 2 * HALVES, slots))
        return pl.pallas_call(
            functools.partial(kernel, stages_of, groups),
            out_shape=(out, out),
            in_specs=[smem] * 4 + [vmem] * 4,
            out_specs=(vmem, vmem),
            scratch_shapes=[
                pltpu.VMEM((2 * rows, features), jnp.bfloat16),
                pltpu.VMEM(wide, jnp.float32),
                pltpu.VMEM((REDUCTIONS,) + wide, jnp.float32),
                pltpu.VMEM(wide, jnp.float32),
                pltpu.VMEM(wide, jnp.float32),
                pltpu.VMEM((2 * rows, columns), jnp.bfloat16),
                pltpu.VMEM((2 * rows, columns), jnp.bfloat16),
                pltpu.VMEM((features, columns), jnp.bfloat16),
                pltpu.VMEM((features, columns), jnp.bfloat16),
            ]
            + [pltpu.VMEM((REDUCTIONS, 2, spot, LANES), jnp.float32) for spot in spots]
            + [semaphores, semaphores],
            compiler_params=pltpu.CompilerParams(
                collective_id=0, has_side_effects=True, vmem_limit_bytes=60 * 1024 * 1024
            ),
        )(counts, damping, eig_low, eig_high, x_first, x_second, w_first, w_second)

    both = ("row", "col")
    return jax.shard_map(
        body,
        mesh=mesh,
        in_specs=(P(None, both), P(None, both), P(both, None), P(both, None), P(), P(), P(), P()),
        out_specs=(P(both, None), P(both, None)),
        check_vma=False,
    )
```

time: 441 us -> 113 us (0.26)
  waiting for transfers between devices: 396 us -> 0 us
  Pallas kernels: 0 us -> 104 us
  matrix products: 24.1 us -> 0 us
  between operations: 17.4 us -> 2.59 us
  local copies, waits for them, and re-layouts: 1.35 us -> 6.46 us
    psum x3 -> x0, waiting for transfers between devices: 396 us -> none  [the longest x2 263 us: body(): lax.psum((high_dot(dense_first, direction), high_dot(dense_second, direct...]
    pallas_call x0 -> x1, Pallas kernels: none -> 104 us  [body(): pl.pallas_call(functools.partial(kernel, stages_of, groups), out_shape=(o...]
    dot_general x12 -> x0, matrix products: 24.1 us -> none  [the longest x6 11 us: back_project(): lax.dot_general(dense, summed, CONTRACT, precision=lax.Precision.HIGHEST,...]
    unnamed x14 -> x8, local copies, waits for them, and re-layouts: 0.04 us -> 6.46 us
  transfers between devices with their start and end apart: 3 -> 0, of which waited for: 3 -> 0; matrix products, arithmetic and copies ran while one was open for 0% -> 0% of each run, Pallas kernels for 0% -> 0%
where the time goes in v1:
time: 113 us
  Pallas kernels  104 us (92%)
  local copies, waits for them, and re-layouts  6.46 us (6%)
  between operations  2.59 us (2%)
    pallas_call x1, Pallas kernels, body(): pl.pallas_call(functools.partial(kernel, stages_of, groups), out_shape=(o...  104 us
    unnamed x8, local copies, waits for them, and re-layouts  6.46 us

profile of v1, /device:TPU:0, one launch (start us, length us, event | category | flops | bytes accessed | tf_op | source)
XLA Modules:
  0.0 113.0 jit_solution(203387002880740407)
XLA Ops:
  2.6 0.0 copy-start
  2.6 2.3 %copy.10.x_first = bf16[768,576]{1,0:T(8,128)(2,1)} copy(bf16[768,576]{0,1:T(8,128)(2,1)} %param.8) | data formatting | bytes 1769472 | tf_op args[0]
  4.9 0.0 copy-done
  4.9 1.3 %copy.11.x_second = bf16[768,576]{1,0:T(8,128)(2,1)} copy(bf16[768,576]{0,1:T(8,128)(2,1)S(1)} %copy-done) | data formatting | bytes 1769472 | tf_op args[1]
  6.2 104.0 %shard_map.95 = (f32[576,256]{1,0:T(8,128)}, f32[576,256]{1,0:T(8,128)}) custom-call(s32[2]{0:T(128)} %counts.1, f32[1]{0:T(128)S(6)} %copy.14.damping, f32[1]{0:T(128)S(6)} %copy.15.eig_low, f32[1]{0:T(128)S(6)} %copy.16.eig_high, bf16[768,576]{1,0:T(8,128)(2,1)} %copy.10.x_first, bf16[768,576]{1,0:T(8,128)(2,1)} %copy.11.x_second, ...), custom_call_target="tpu_custom_call" | custom-call | tf_op jit(solution)/shard_map/pallas_call | solution.py:280
  110.2 0.0 copy-start.1
  110.2 2.0 %copy.17 = f32[576,256]{1,0:T(8,128)} copy(f32[576,256]{1,0:T(8,128)} %get-tuple-element.4) | data formatting | bytes 1179648
  112.2 0.0 copy-done.1
  112.2 0.8 copy.18
Async XLA Ops:
  2.6 2.3 %copy-start = (bf16[768,576]{0,1:T(8,128)(2,1)S(1)}, bf16[768,576]{0,1:T(8,128)(2,1)}, u32[]{:S(2)}) copy-start(bf16[768,576]{0,1:T(8,128)(2,1)} %param.9) | copy-start | bytes 2654212
  110.2 2.0 %copy-start.1 = (f32[576,256]{1,0:T(8,128)S(1)}, f32[576,256]{1,0:T(8,128)}, u32[]{:S(2)}) copy-start(f32[576,256]{1,0:T(8,128)} %get-tuple-element.5) | copy-start | bytes 1769476

commit v2 on v1

v2 whole, which is shorter than its diff:
```python
import functools

import jax
import jax.numpy as jnp
from jax import lax
from jax.experimental import pallas as pl
from jax.experimental.pallas import tpu as pltpu
from jax.sharding import PartitionSpec as P

ITERS = 2
HALVES = 2
LANES = 128
SUBLANES = 8
REDUCTIONS = ITERS + 1
LEVELS = 32760.0
TINY = 1e-30


def axis_groups(name, size):
    pair = 2 if size % 2 == 0 else 1
    found = [(name, 1, pair), (name, pair, size // pair)]
    return [group for group in found if group[2] > 1]


def joined(parts):
    members = 1
    for part in parts:
        members *= part[2]
    return [(tuple(parts), None, members)] if members > 1 else []


def plan(mesh_shape, rows):
    col = axis_groups("col", mesh_shape["col"])
    row = axis_groups("row", mesh_shape["row"])
    order = joined(col[:1]) + joined(row[:1] + col[1:]) + joined(row[1:])
    orders = [order] * HALVES
    result = []
    for order in orders:
        height, stages = rows, []
        for group in order:
            members = group[2]
            split = height % (members * SUBLANES) == 0
            chunk = height // members if split else height
            stages.append((group, height, chunk, split))
            height = chunk
        result.append(stages)
    return result


def member_of(group):
    index, weight = 0, 1
    for name, stride, members in group[0]:
        index = index + lax.rem(lax.div(lax.axis_index(name), stride), members) * weight
        weight *= members
    return index


def peer_at(group, offset):
    device, index, weight = {}, 0, 1
    for name, stride, members in group[0]:
        me = lax.rem(lax.div(lax.axis_index(name), stride), members)
        other = lax.rem(me + offset % members, members)
        device[name] = device.get(name, lax.axis_index(name)) + (other - me) * stride
        index = index + other * weight
        offset, weight = offset // members, weight * members
    return device, index


def kernel(
    stages_of, groups, counts, damping, eig_low, eig_high, x_first, x_second, w_first, w_second,
    merged, residual, dense, turned, sums, coded, steps, d_zero, rest, pieces, q_pieces, *more,
):
    depth = max(len(stages) for stages in stages_of)
    outgoing, landing = more[:depth], more[depth : 2 * depth]
    out_steps, in_steps, send_sem, recv_sem = more[2 * depth :]
    rows = x_first.shape[0]
    final = stages_of[0][-1][2]

    barrier = pltpu.get_barrier_semaphore()
    partners = 0
    for group in groups:
        for offset in range(1, group[2]):
            pl.semaphore_signal(
                barrier, inc=1, device_id=peer_at(group, offset)[0], device_id_type=pl.DeviceIdType.MESH
            )
            partners += 1

    def lane(value):
        return jnp.full((1, LANES), value, jnp.float32)

    scales = [1.0 / lane(counts[i].astype(jnp.float32)) for i in range(2)]
    ridge = lane(damping[0])
    middle = (lane(eig_high[0]) + lane(eig_low[0])) / 2.0
    radius = (lane(eig_high[0]) - lane(eig_low[0])) / 2.0
    sigma = middle / radius

    position = lax.broadcasted_iota(jnp.int32, x_first.shape, 0)
    for domain, source in enumerate((x_first, x_second)):
        value = source[...].astype(jnp.float32)
        dense[pl.ds(domain * rows, rows), :] = jnp.where(position < counts[domain], value, 0.0).astype(jnp.bfloat16)

    def reduce_all(index, produce):
        sent = []
        parts = [(domain, half) for domain in range(2) for half in range(HALVES)]

        def start(part, slot, src, dst, device):
            at = (index, part, slot)
            copy = pltpu.make_async_remote_copy(
                src_ref=src, dst_ref=dst, send_sem=send_sem.at[at], recv_sem=recv_sem.at[at],
                device_id=device, device_id_type=pl.DeviceIdType.MESH,
            )
            copy.start()
            return copy

        state = {}

        def launch_scatter(part, stage):
            domain, half = parts[part]
            group, height, chunk, split = stages_of[half][stage]
            base = state[part]["base"]
            copies = []
            for offset in range(1, group[2]):
                device, other = peer_at(group, offset)
                begin = domain * rows + base + (other * chunk if split else 0)
                slot = state[part]["slot"] + offset - 1
                value = sums[half, pl.ds(pl.multiple_of(begin, SUBLANES), chunk), :]
                outgoing[stage][part, offset - 1, pl.ds(0, chunk), :], out_steps[part, slot] = fixed(value)
                held, room = outgoing[stage], landing[stage]
                copies.append(
                    start(
                        part, slot,
                        held.at[part, offset - 1, pl.ds(0, chunk), :],
                        room.at[index, part, offset - 1, pl.ds(0, chunk), :],
                        device,
                    )
                )
                copies.append(
                    start(len(parts) + part, slot, out_steps.at[part, slot], in_steps.at[index, part, slot], device)
                )
            sent.extend(copies)
            state[part]["wait"] = copies

        def finish_scatter(part, stage):
            domain, half = parts[part]
            group, height, chunk, split = stages_of[half][stage]
            st = state[part]
            st["bases"].append(st["base"])
            if split:
                st["base"] = st["base"] + member_of(group) * chunk
            own = pl.ds(pl.multiple_of(domain * rows + st["base"], SUBLANES), chunk)
            for copy in st["wait"]:
                copy.wait_recv()
            total = sums[half, own, :]
            for offset in range(1, group[2]):
                sent_here = landing[stage][index, part, offset - 1, pl.ds(0, chunk), :]
                total = total + sent_here.astype(jnp.int32).astype(jnp.float32) * in_steps[index, part, st["slot"] + offset - 1]
            if stage == len(stages_of[half]) - 1:
                st["total"] = total
            else:
                sums[half, own, :] = total
            st["slot"] += group[2] - 1

        def fixed(value):
            top = jnp.maximum(jnp.max(jnp.abs(value), axis=0, keepdims=True), TINY)
            return jnp.round(value * (LEVELS / top)).astype(jnp.int32).astype(jnp.int16), top * (1.0 / LEVELS)

        def encode(half):
            pair = jnp.concatenate([state[half]["total"], state[HALVES + half]["total"]], axis=0)
            mine = lax.div(state[half]["base"], final)
            coded[index, half, mine], steps[index, half, mine] = fixed(pair)

        def launch_gather(half, stage):
            group, height, chunk, split = stages_of[half][stage]
            st = state[half]
            st["slot"] -= group[2] - 1
            copies = []
            if split:
                where = pl.ds(lax.div(st["base"], final), chunk // final)
                for offset in range(1, group[2]):
                    device, _ = peer_at(group, offset)
                    slot = st["slot"] + offset - 1
                    for phase, held in ((0, coded), (1, steps)):
                        place = held.at[index, half, where]
                        copies.append(start(2 * len(parts) + 2 * half + phase, slot, place, place, device))
            st["base"] = st["bases"].pop()
            sent.extend(copies)
            st["wait"] = copies

        def finish_gather(half):
            for copy in state[half]["wait"]:
                copy.wait_recv()

        count = [len(stages_of[half]) for _, half in parts]
        for domain in range(2):
            produce(domain)
            if index == 0 and domain == 0:
                pl.semaphore_wait(barrier, partners)
            for half in range(HALVES):
                part = domain * HALVES + half
                state[part] = {"base": 0, "slot": 0, "bases": []}
                launch_scatter(part, 0)
        if index == 0:
            turned[...] = dense[...].T
        for stage in range(max(count)):
            for part in range(len(parts)):
                if stage < count[part]:
                    finish_scatter(part, stage)
                    if stage + 1 < count[part]:
                        launch_scatter(part, stage + 1)
                    elif part >= HALVES:
                        encode(part - HALVES)
                        launch_gather(part - HALVES, stage)
        for stage in reversed(range(max(count))):
            for half in range(HALVES):
                if stage < count[half]:
                    finish_gather(half)
                    if stage > 0:
                        launch_gather(half, stage - 1)
        return sent

    def summed(index, domain, half):
        value = coded[index, half].astype(jnp.int32).astype(jnp.float32) * steps[index, half]
        return value[:, domain * final : (domain + 1) * final, :].reshape(rows, LANES)

    def settle(sent):
        for copy in sent:
            copy.wait_send()

    def split_store(domain, half, value):
        place = pl.ds(domain * rows, rows)
        top = value.astype(jnp.bfloat16)
        pieces[place, pl.ds(half * LANES, LANES)] = top
        pieces[place, pl.ds((HALVES + half) * LANES, LANES)] = (value - top.astype(jnp.float32)).astype(jnp.bfloat16)

    def back_project():
        both = jnp.dot(turned[...], pieces[...], preferred_element_type=jnp.float32)
        return both[:, : HALVES * LANES] + both[:, HALVES * LANES :]

    def store_sums(domain, value):
        for half in range(HALVES):
            sums[half, pl.ds(domain * rows, rows), :] = value[:, half * LANES : (half + 1) * LANES]

    def first_product(domain):
        weights = (w_first, w_second)[domain]
        store_sums(
            domain,
            jnp.dot(dense[pl.ds(domain * rows, rows), :], weights[...], preferred_element_type=jnp.float32),
        )

    def next_product(domain):
        both = jnp.dot(dense[pl.ds(domain * rows, rows), :], q_pieces[...], preferred_element_type=jnp.float32)
        store_sums(domain, both[:, : HALVES * LANES] + both[:, HALVES * LANES :])

    def project_and_sum(index):
        seen = back_project()
        top = seen.astype(jnp.bfloat16)
        q_pieces[:, : HALVES * LANES] = top
        q_pieces[:, HALVES * LANES :] = (seen - top.astype(jnp.float32)).astype(jnp.bfloat16)
        if index == 1:
            merged[...] = seen
        else:
            merged[...] = merged[...] + seen
        return reduce_all(index, next_product)

    sent = reduce_all(0, first_product)
    settle(sent)
    blocks = [(domain, half, pl.ds(domain * rows, rows)) for domain in range(2) for half in range(HALVES)]
    for domain, half, place in blocks:
        value = summed(0, domain, half) * scales[domain]
        rest[half, place, :] = value
        value = value / middle
        d_zero[half, place, :] = value
        split_store(domain, half, value)
    rho_now = 1.0 / sigma
    for step in range(ITERS):
        settle(project_and_sum(step + 1))
        rho_new = 1.0 / (2.0 * sigma - rho_now)
        for domain, half, place in blocks:
            direction = d_zero[half, place, :]
            left = rest[half, place, :] - (summed(step + 1, domain, half) * scales[domain] + ridge * direction)
            if step + 1 < ITERS:
                rest[half, place, :] = left
                direction = rho_new * rho_now * direction + (2.0 * rho_new / radius) * left
                d_zero[half, place, :] = direction
                split_store(domain, half, direction)
            else:
                split_store(domain, half, left)
        rho_now = rho_new
    residual[...] = back_project()


def solution(mesh):
    shape = dict(mesh.shape)

    def body(x_first, x_second, w_first, w_second, counts, damping, eig_low, eig_high):
        rows, features = x_first.shape
        columns = w_first.shape[1]
        stages_of = plan(shape, rows)
        groups = [stage[0] for stage in stages_of[0]]
        slots = max(sum(stage[0][2] - 1 for stage in stages) for stages in stages_of)
        levels = [
            (max(stages[at][0][2] for stages in stages_of) - 1, max(stages[at][2] for stages in stages_of), LANES)
            for at in range(len(stages_of[0]))
        ]
        final = stages_of[0][-1][2]
        blocks = rows // final
        smem = pl.BlockSpec(memory_space=pltpu.SMEM)
        vmem = pl.BlockSpec(memory_space=pltpu.VMEM)
        out = jax.ShapeDtypeStruct((features, columns), jnp.float32)
        wide = (HALVES, 2 * rows, LANES)
        semaphores = pltpu.SemaphoreType.DMA((REDUCTIONS, 6 * HALVES, slots))
        return pl.pallas_call(
            functools.partial(kernel, stages_of, groups),
            out_shape=(out, out),
            in_specs=[smem] * 4 + [vmem] * 4,
            out_specs=(vmem, vmem),
            scratch_shapes=[
                pltpu.VMEM((2 * rows, features), jnp.bfloat16),
                pltpu.VMEM((features, 2 * rows), jnp.bfloat16),
                pltpu.VMEM(wide, jnp.float32),
                pltpu.VMEM((REDUCTIONS, HALVES, blocks, 2 * final, LANES), jnp.int16),
                pltpu.VMEM((REDUCTIONS, HALVES, blocks, 1, LANES), jnp.float32),
                pltpu.VMEM(wide, jnp.float32),
                pltpu.VMEM(wide, jnp.float32),
                pltpu.VMEM((2 * rows, 2 * columns), jnp.bfloat16),
                pltpu.VMEM((features, 2 * columns), jnp.bfloat16),
            ]
            + [pltpu.VMEM((2 * HALVES,) + level, jnp.int16) for level in levels]
            + [pltpu.VMEM((REDUCTIONS, 2 * HALVES) + level, jnp.int16) for level in levels]
            + [
                pltpu.VMEM((2 * HALVES, slots, 1, LANES), jnp.float32),
                pltpu.VMEM((REDUCTIONS, 2 * HALVES, slots, 1, LANES), jnp.float32),
            ]
            + [semaphores, semaphores],
            compiler_params=pltpu.CompilerParams(
                collective_id=0, has_side_effects=True, vmem_limit_bytes=60 * 1024 * 1024
            ),
        )(counts, damping, eig_low, eig_high, x_first, x_second, w_first, w_second)

    both = ("row", "col")
    return jax.shard_map(
        body,
        mesh=mesh,
        in_specs=(P(None, both), P(None, both), P(both, None), P(both, None), P(), P(), P(), P()),
        out_specs=(P(both, None), P(both, None)),
        check_vma=False,
    )
```

time: 113 us -> 95.9 us (0.85)
  Pallas kernels: 104 us -> 86.6 us
    pallas_call x1, Pallas kernels: 104 us -> 86.6 us  [body(): pl.pallas_call(functools.partial(kernel, stages_of, groups), out_shape=(o...]
where the time goes in v2:
time: 95.9 us; the launch traced here: 95.7 us
  Pallas kernels  86.6 us (90%)
  local copies, waits for them, and re-layouts  6.46 us (7%)
  between operations  2.59 us (3%)
    pallas_call x1, Pallas kernels, body(): pl.pallas_call(functools.partial(kernel, stages_of, groups), out_shape=(o...  86.6 us
    unnamed x8, local copies, waits for them, and re-layouts  6.46 us

profile of v2, /device:TPU:0, one launch (start us, length us, event | category | flops | bytes accessed | tf_op | source)
XLA Modules:
  0.0 95.7 jit_solution(206946173780384741)
XLA Ops:
  2.6 0.0 copy-start
  2.6 2.3 %copy.10.x_first = bf16[768,576]{1,0:T(8,128)(2,1)} copy(bf16[768,576]{0,1:T(8,128)(2,1)} %param.8) | data formatting | bytes 1769472 | tf_op args[0]
  4.9 0.0 copy-done
  4.9 1.3 %copy.11.x_second = bf16[768,576]{1,0:T(8,128)(2,1)} copy(bf16[768,576]{0,1:T(8,128)(2,1)S(1)} %copy-done) | data formatting | bytes 1769472 | tf_op args[1]
  6.2 86.6 %shard_map.95 = (f32[576,256]{1,0:T(8,128)}, f32[576,256]{1,0:T(8,128)}) custom-call(s32[2]{0:T(128)} %counts.1, f32[1]{0:T(128)S(6)} %copy.14.damping, f32[1]{0:T(128)S(6)} %copy.15.eig_low, f32[1]{0:T(128)S(6)} %copy.16.eig_high, bf16[768,576]{1,0:T(8,128)(2,1)} %copy.10.x_first, bf16[768,576]{1,0:T(8,128)(2,1)} %copy.11.x_second, ...), custom_call_target="tpu_custom_call" | custom-call | tf_op jit(solution)/shard_map/pallas_call | solution.py:312
  92.9 0.0 copy-start.1
  92.9 2.0 %copy.17 = f32[576,256]{1,0:T(8,128)} copy(f32[576,256]{1,0:T(8,128)} %get-tuple-element.4) | data formatting | bytes 1179648
  94.9 0.0 copy-done.1
  94.9 0.8 copy.18
Async XLA Ops:
  2.6 2.3 %copy-start = (bf16[768,576]{0,1:T(8,128)(2,1)S(1)}, bf16[768,576]{0,1:T(8,128)(2,1)}, u32[]{:S(2)}) copy-start(bf16[768,576]{0,1:T(8,128)(2,1)} %param.9) | copy-start | bytes 2654212
  92.9 2.0 %copy-start.1 = (f32[576,256]{1,0:T(8,128)S(1)}, f32[576,256]{1,0:T(8,128)}, u32[]{:S(2)}) copy-start(f32[576,256]{1,0:T(8,128)} %get-tuple-element.5) | copy-start | bytes 1769476
